TPU v7x, 256 devices: a whole 4x4x8 slice. The times are simulated.
256 devices in a mesh: expert: 32 (over x, z), vocab: 8 (over y, core).
Axes of the slice: x: 4, y: 4, z: 8, core: 2. Of those that a mesh axis runs over, the one named last changes fastest.
Arguments:
- out_grad: bfloat16 [4096, 4096], P('expert', 'vocab'), may hold values from -6 to 6
- residual_stream: bfloat16 [4096, 4096], P('expert', 'vocab'), may hold values from -228 to 228
- norm_gain: float32 [4096], P('vocab'), may hold values from 0.25 to 51
- expert_ids: int32 [4096, 8], P('expert'), may hold values from 0 to 31, all different within a row; in each aligned block of 128 rows (0 to 127, 128 to 255, ...) at most 38 rows name the same one
- gate_scores: float32 [4096, 8], P('expert'), may hold values from 0.05 to 1
- saved_gate: bfloat16 [32, 1216, 1536], P('expert', None, 'vocab'), may hold values from -6 to 6
- saved_up: bfloat16 [32, 1216, 1536], P('expert', None, 'vocab'), may hold values from -6 to 6
- gate_weight: bfloat16 [32, 4096, 1536], P('expert', None, 'vocab'), may hold values from -0.09375 to 0.09375
- up_weight: bfloat16 [32, 4096, 1536], P('expert', None, 'vocab'), may hold values from -0.09375 to 0.09375
- down_weight: bfloat16 [32, 1536, 4096], P('expert', 'vocab'), may hold values from -0.15625 to 0.15625
- embedding: bfloat16 [98304, 4096], P(('expert', 'vocab')), may hold values from -0.09375 to 0.09375
- allowed: int32 [98304], P(('expert', 'vocab')), may hold values 0 or 1
- suffix_start: int32 [32], P('expert'), may hold values from 0 to 108
Outputs:
- token_grad: bfloat16 [4096, 4096], P('expert', 'vocab')
- scores: float32 [640, 98304], P(None, ('expert', 'vocab'))
Inputs may be any that keep to these rules, and one draw needn't show every extreme that they name: `expert_ids`: in each aligned block of 128 rows (one behavior) a row names 8 different experts and no expert is named by more than 38 rows; some expert is named by exactly 38 rows in some blocks.
All inputs are finite; a program needn't handle non-finite values. No bound on the sum of `allowed` on one device may be relied on, other than what follows from the above.
Results may differ from a plain program's by a relative error of at most 0.01.
Values may be sent and summed in bfloat16 or wider, within the bound.
No kernel may reach another device: no remote copies, remote signals or barrier semaphores. Data moves between devices by JAX's collectives and lax.ppermute only.
A program may use at most 128 MiB of HBM per device.

v0:
```python
import jax
import jax.numpy as jnp
from jax import lax
from jax.sharding import PartitionSpec as P

D = 4096
SUFFIX = 20


def sent_to_all(value, axis):
    peers = lax.axis_size(axis)
    return lax.all_to_all(
        jnp.broadcast_to(value[None], (peers, *value.shape)), axis, 0, 0, tiled=True
    )


def taken_together(value, axis):
    everything = sent_to_all(value, axis)
    return jnp.sum(everything, axis=0)


def in_order(parts, dim):
    parts = jnp.moveaxis(parts, 0, dim)
    lengths = parts.shape
    return parts.reshape(*lengths[:dim], lengths[dim] * lengths[dim + 1], *lengths[dim + 2 :])


def collect(value, axis, dim):
    return in_order(sent_to_all(value, axis), dim)


def shards(
    out_grad,
    residual_stream,
    norm_gain,
    expert_ids,
    gate_scores,
    saved_gate,
    saved_up,
    gate_weight,
    up_weight,
    down_weight,
    embedding,
    allowed,
    suffix_start,
):
    n_expert = lax.axis_size("expert")
    seq_len, d_slice = out_grad.shape
    top_k = expert_ids.shape[1]
    slot_count = saved_gate.shape[1]
    capacity = slot_count // n_expert
    contract = (((1,), (1,)), ((), ()))
    chosen = expert_ids.reshape(-1)
    matches = (chosen[:, None] == jnp.arange(n_expert, dtype=jnp.int32)[None, :]).astype(jnp.int32)
    before = jnp.cumsum(matches, axis=0) - matches
    position = jnp.sum(before * matches, axis=1)
    target = chosen * capacity + position
    gate_share = gate_scores / jnp.sum(gate_scores, axis=1, keepdims=True)
    routed = (gate_share[:, :, None] * out_grad.astype(jnp.float32)[:, None, :]).astype(
        jnp.bfloat16
    )
    routed = routed.reshape(seq_len * top_k, d_slice)
    buffer = jnp.zeros((slot_count, d_slice), jnp.bfloat16).at[target].set(routed)
    arrived = lax.all_to_all(buffer, "expert", split_axis=0, concat_axis=0, tiled=True)
    incoming = lax.all_gather(arrived, "vocab", axis=1, tiled=True)
    act_grad = lax.dot_general(
        incoming, down_weight[0], contract, preferred_element_type=jnp.float32
    )
    pre_gate = saved_gate[0].astype(jnp.float32)
    pre_up = saved_up[0].astype(jnp.float32)
    sigmoid_g = jax.nn.sigmoid(pre_gate)
    gate_grad = (act_grad * pre_up * sigmoid_g * (1.0 + pre_gate * (1.0 - sigmoid_g))).astype(
        jnp.bfloat16
    )
    up_grad = (act_grad * pre_gate * sigmoid_g).astype(jnp.bfloat16)
    partial_value = lax.dot_general(
        gate_grad, gate_weight[0], contract, preferred_element_type=jnp.float32
    )
    partial_value = partial_value + lax.dot_general(
        up_grad, up_weight[0], contract, preferred_element_type=jnp.float32
    )
    partial_rounded = partial_value.astype(jnp.bfloat16)
    slot_grad = lax.psum_scatter(partial_rounded, "vocab", scatter_dimension=1, tiled=True).astype(
        jnp.float32
    )
    returned = lax.all_to_all(
        slot_grad.astype(jnp.bfloat16), "expert", split_axis=0, concat_axis=0, tiled=True
    ).astype(slot_grad.dtype)
    moe_grad = jnp.sum(returned[target].reshape(seq_len, top_k, d_slice), axis=1)
    resid = residual_stream.astype(jnp.float32)
    sum_squares = taken_together(jnp.sum(resid * resid, axis=1), "vocab")
    inverse = lax.rsqrt(sum_squares / D + 1e-06)
    normed = resid * inverse[:, None]
    scaled = moe_grad * norm_gain[None, :]
    row_project = taken_together(jnp.sum(scaled * normed, axis=1), "vocab") / D
    token_grad = (
        out_grad.astype(jnp.float32) + inverse[:, None] * (scaled - normed * row_project[:, None])
    ).astype(jnp.bfloat16)
    suffix_grad = lax.dynamic_slice_in_dim(token_grad, suffix_start[0], SUFFIX, 0)
    suffix_grad = collect(suffix_grad, "vocab", 1)
    raw_scores = -lax.dot_general(
        lax.all_gather(suffix_grad, "expert", axis=0, tiled=True),
        embedding,
        contract,
        preferred_element_type=jnp.float32,
    )
    scores = jnp.where(allowed[None, :] > 0, raw_scores, jnp.float32(0.0))
    return (token_grad, scores)


def solution(mesh):
    placed = (
        P("expert", "vocab"),
        P("expert", "vocab"),
        P("vocab"),
        P("expert", None),
        P("expert", None),
        P("expert", None, "vocab"),
        P("expert", None, "vocab"),
        P("expert", None, "vocab"),
        P("expert", None, "vocab"),
        P("expert", "vocab", None),
        P(("expert", "vocab"), None),
        P(("expert", "vocab")),
        P("expert"),
    )
    return jax.shard_map(
        shards,
        mesh=mesh,
        in_specs=placed,
        out_specs=(P("expert", "vocab"), P(None, ("expert", "vocab"))),
        check_vma=False,
    )
```

profile of v0, /device:TPU:8, one launch (start us, length us, event | category | flops | bytes accessed | tf_op | source)
XLA Modules:
  0.0 413.3 jit_solution(6126934621142170420)
XLA Ops:
  7.2 0.9 copy.37
  8.2 0.1 eq.29
  8.3 0.1 eq.25
  8.3 0.7 broadcast_multiply_fusion
  9.1 9.0 %reduce-window.6 = s32[32,8,128]{2,1,0:T(8,128)S(1)} reduce-window(s32[32,8,128]{2,1,0:T(8,128)S(1)} %fusion.39, s32[]{:T(128)} %constant.7.clone.1), window={size=1x1x128 pad=0_0x0_0x127_0}, to_apply=%region_2.3 | reduce-window | flops 4161536 | bytes 262148 | tf_op jit(solution)/shard_map/reduce-window
  18.1 0.1 slice.10
  18.2 0.1 copy.39
  18.3 0.1 copy.40
  18.4 0.1 broadcast_add_fusion
  18.5 0.1 copy.36
  18.6 0.1 mul.95
  18.7 0.9 convert_element_type.50
  19.7 0.7 reduce_sum.69
  20.4 0.7 broadcast_divide_fusion
  21.0 0.7 copy.41
  21.8 0.9 mul.97
  22.8 6.6 %scatter_custom_fusion = bf16[1216,512]{1,0:T(8,128)(2,1)} fusion(s32[1024]{0:T(1024)S(1)} %bitcast.66, f32[128,512]{1,0:T(8,128)S(1)} %convert_element_type.50, f32[1024]{0:T(1024)S(1)} %mul.97, bf16[]{:T(256)} %constant.5.clone.1), kind=kCustom, calls=%fused_computation.16 | custom fusion | flops 1048576 | bytes 1511426 | tf_op jit(solution)/shard_map/scatter | solution.py:63
  29.4 2.3 all_to_all.26
  31.7 46.4 %all_to_all.38 = bf16[32,38,512]{2,1,0:T(8,128)(2,1)} all-to-all(bf16[32,38,512]{2,1,0:T(8,128)(2,1)} %all_to_all.26), channel_id=1, replica_groups=mesh['expert'=32,'vocab'=8] {'expert'}, dimensions={0} | all-to-all | bytes 2490368 | tf_op jit(solution)/shard_map/all_to_all | solution.py:64
  78.1 2.3 all_to_all.28
  80.4 54.2 %all-gather.4.cloned.1.call-done = bf16[1216,4096]{1,0:T(8,128)(2,1)} async-done(((bf16[1216,512]{1,0:T(8,128)(2,1)}), bf16[1216,4096]{1,0:T(8,128)(2,1)}) %all-gather.4.cloned.1.call-update) | async-done | bytes 9961488 | tf_op jit(solution)/shard_map/all_gather | solution.py:65
  134.6 7.6 %fusion.4 = f32[1216,192]{0,1:T(8,128)S(1)} fusion(bf16[1216,4096]{1,0:T(8,128)(2,1)} %all-gather.4.cloned.1.call-done, bf16[1,192,4096]{2,1,0:T(8,128)(2,1)} %param.22), kind=kOutput, calls=%fused_computation.9 | convolution fusion | flops 1912602624 | bytes 12468224 | tf_op jit(solution)/shard_map/dot_general | solution.py:66
  142.2 0.9 copy-done.1
  143.2 8.4 %fusion.2 = f32[1216,4096]{1,0:T(8,128)} fusion(bf16[1,4096,192]{1,2,0:T(8,128)(2,1)S(1)} %copy-done.3, f32[1216,192]{0,1:T(8,128)S(1)} %fusion.4, bf16[1,1216,192]{1,2,0:T(8,128)(2,1)S(1)} %copy-done.5, bf16[1,1216,192]{1,2,0:T(8,128)(2,1)S(1)} %copy-done.2), kind=kOutput, calls=%fused_computation.7 | convolution fusion | flops 1915404288 | bytes 23363584 | tf_op jit(solution)/shard_map/dot_general | solution.py:76
  151.6 14.2 %add_convert_fusion = bf16[1216,4096]{1,0:T(8,128)(2,1)} fusion(f32[1216,4096]{1,0:T(8,128)} %fusion.2, bf16[1,4096,192]{1,2,0:T(8,128)(2,1)} %param.21, f32[1216,192]{0,1:T(8,128)} %copy-done.1, bf16[1,1216,192]{1,2,0:T(8,128)(2,1)} %param.18), kind=kOutput, calls=%fused_computation.2 | convolution fusion | flops 1924198400 | bytes 32858112 | tf_op jit(solution)/shard_map/dot_general | solution.py:79
  165.7 0.9 copy-done.4
  166.6 0.1 fusion.35
  166.7 0.6 broadcast_in_dim.16
  167.3 4.5 %all-to-all-start = ((f32[8,1,128]{2,1,0:T(1,128)}), f32[8,1,128]{2,1,0:T(1,128)S(1)}, u32[]{:S(2)}, u32[]{:S(2)}) async-start(f32[8,1,128]{2,1,0:T(1,128)} %broadcast_in_dim.16), calls=%async_computation | async-start | bytes 8192 | tf_op jit(solution)/shard_map/all_to_all | solution.py:12
  171.9 55.1 %reduce-scatter.2.cloned.1.call-done = bf16[1216,512]{1,0:T(8,128)(2,1)} async-done(((bf16[1216,4096]{1,0:T(8,128)(2,1)}), bf16[1216,512]{1,0:T(8,128)(2,1)}) %reduce-scatter.2.cloned.1.call-update) | async-done | bytes 1245200 | tf_op jit(solution)/shard_map/reduce_scatter | solution.py:83
  227.0 2.3 all_to_all.29
  229.3 10.2 %all-to-all-start.2 = ((bf16[32,38,512]{2,1,0:T(8,128)(2,1)}), bf16[32,38,512]{2,1,0:T(8,128)(2,1)}, u32[]{:S(2)}, u32[]{:S(2)}) async-start(bf16[32,38,512]{2,1,0:T(8,128)(2,1)} %all_to_all.29), calls=%async_computation.3 | async-start | bytes 2621440 | tf_op jit(solution)/shard_map/all_to_all | solution.py:86
  239.5 34.5 %all-to-all-done.2 = bf16[32,38,512]{2,1,0:T(8,128)(2,1)} async-done(((bf16[32,38,512]{2,1,0:T(8,128)(2,1)}), bf16[32,38,512]{2,1,0:T(8,128)(2,1)}, u32[]{:S(2)}, u32[]{:S(2)}) %all-to-all-start.2) | async-done | bytes 1245216 | tf_op jit(solution)/shard_map/all_to_all | solution.py:86
  274.0 2.7 reshape.102
  276.7 7.0 %gather_fusion = f32[1024,512]{1,0:T(8,128)} fusion(f32[1216,512]{1,0:T(8,128)} %reshape.102, s32[1024]{0:T(1024)S(1)} %broadcast_clamp_fusion), kind=kCustom, calls=%fused_computation | custom fusion | bytes 4198400 | tf_op jit(solution)/shard_map/gather | solution.py:89
  283.6 2.1 bitcast_reduce_fusion
  285.8 0.2 fusion.30
  286.0 0.6 broadcast_in_dim.18
  286.6 5.1 %all-to-all-start.3 = ((f32[8,1,128]{2,1,0:T(1,128)}), f32[8,1,128]{2,1,0:T(1,128)S(1)}, u32[]{:S(2)}, u32[]{:S(2)}) async-start(f32[8,1,128]{2,1,0:T(1,128)} %broadcast_in_dim.18), calls=%async_computation.4 | async-start | bytes 8192 | tf_op jit(solution)/shard_map/all_to_all | solution.py:12
  292.4 3.1 all-to-all-done.3
  295.5 0.5 reduce_sum.72
  296.0 0.7 broadcast_multiply_fusion.1
  296.6 1.1 fusion.34
  297.8 9.2 %all_to_all.39 = bf16[8,20,512]{2,1,0:T(8,128)(2,1)S(1)} all-to-all(bf16[8,20,512]{2,1,0:T(8,128)(2,1)S(1)} %broadcast_in_dim.20), channel_id=1, replica_groups=mesh['expert'=32,'vocab'=8] {'vocab'}, dimensions={0} | all-to-all | bytes 327680 | tf_op jit(solution)/shard_map/all_to_all | solution.py:12
  307.0 0.8 reshape.119
  307.9 84.7 %all-gather.6.cloned.1.call-done = bf16[32,20,4096]{2,1,0:T(8,128)(2,1)} async-done(((bf16[1,20,4096]{2,1,0:T(8,128)(2,1)}), bf16[32,20,4096]{2,1,0:T(8,128)(2,1)}) %all-gather.6.cloned.1.call-update) | async-done | bytes 5242896 | tf_op jit(solution)/shard_map/all_gather | solution.py:102
  392.6 7.8 %reshape.120 = bf16[640,4096]{1,0:T(8,128)(2,1)} reshape(bf16[32,20,4096]{2,1,0:T(8,128)(2,1)} %all-gather.6.cloned.1.call-done) | data formatting | bytes 10485760
  400.4 6.3 %fusion.6 = f32[640,384]{1,0:T(8,128)} fusion(bf16[640,4096]{1,0:T(8,128)(2,1)} %reshape.120, bf16[384,4096]{1,0:T(8,128)(2,1)S(1)} %copy-done, pred[384]{0:T(512)(128)(4,1)S(1)} %broadcast_compare_fusion), kind=kOutput, calls=%fused_computation.15 | convolution fusion | flops 2013757440 | bytes 9372032 | tf_op jit(solution)/shard_map/dot_general | solution.py:101
  (35 shorter events, 0.4 us)
Async XLA Ops:
  7.2 393.3 %copy-start = (bf16[384,4096]{1,0:T(8,128)(2,1)S(1)}, bf16[384,4096]{1,0:T(8,128)(2,1)}, u32[]{:S(2)}) copy-start(bf16[384,4096]{1,0:T(8,128)(2,1)} %param.23) | copy-start | bytes 9437188
  7.2 127.4 %all-gather.4.cloned.1.call-start = ((), (), s32[]{:S(2)}) async-start(), calls=%async_computation.6 | async-start | bytes 11206656 | tf_op jit(solution)/shard_map/all_gather | solution.py:65
  80.4 146.6 %reduce-scatter.2.cloned.1.call-start = ((), (), s32[]{:S(2)}) async-start(), calls=%async_computation.7 | async-start | bytes 11206656 | tf_op jit(solution)/shard_map/reduce_scatter | solution.py:83
  134.6 8.6 %copy-start.2 = (bf16[1,1216,192]{1,2,0:T(8,128)(2,1)S(1)}, bf16[1,1216,192]{1,2,0:T(8,128)(2,1)}, u32[]{:S(2)}) copy-start(bf16[1,1216,192]{1,2,0:T(8,128)(2,1)} %param.18) | copy-start | bytes 1400836
  134.6 8.6 %copy-start.3 = (bf16[1,4096,192]{1,2,0:T(8,128)(2,1)S(1)}, bf16[1,4096,192]{1,2,0:T(8,128)(2,1)}, u32[]{:S(2)}) copy-start(bf16[1,4096,192]{1,2,0:T(8,128)(2,1)} %param.20) | copy-start | bytes 4718596
  134.6 8.6 %copy-start.5 = (bf16[1,1216,192]{1,2,0:T(8,128)(2,1)S(1)}, bf16[1,1216,192]{1,2,0:T(8,128)(2,1)}, u32[]{:S(2)}) copy-start(bf16[1,1216,192]{1,2,0:T(8,128)(2,1)} %param.19) | copy-start | bytes 1400836
  142.2 0.9 copy-start.1
  165.7 0.9 copy-start.4
  167.3 62.0 %all-to-all-start = ((f32[8,1,128]{2,1,0:T(1,128)}), f32[8,1,128]{2,1,0:T(1,128)S(1)}, u32[]{:S(2)}, u32[]{:S(2)}) async-start(f32[8,1,128]{2,1,0:T(1,128)} %broadcast_in_dim.16), calls=%async_computation | async-start | bytes 8192 | tf_op jit(solution)/shard_map/all_to_all | solution.py:12
  229.3 44.7 %all-to-all-start.2 = ((bf16[32,38,512]{2,1,0:T(8,128)(2,1)}), bf16[32,38,512]{2,1,0:T(8,128)(2,1)}, u32[]{:S(2)}, u32[]{:S(2)}) async-start(bf16[32,38,512]{2,1,0:T(8,128)(2,1)} %all_to_all.29), calls=%async_computation.3 | async-start | bytes 2621440 | tf_op jit(solution)/shard_map/all_to_all | solution.py:86
  283.6 2.1 copy-start.7
  283.6 24.2 %copy-start.8 = (s32[384]{0:T(512)S(1)}, s32[384]{0:T(512)}, u32[]{:S(2)}) copy-start(s32[384]{0:T(512)} %param.24) | copy-start | bytes 4612
  286.6 8.9 %all-to-all-start.3 = ((f32[8,1,128]{2,1,0:T(1,128)}), f32[8,1,128]{2,1,0:T(1,128)S(1)}, u32[]{:S(2)}, u32[]{:S(2)}) async-start(f32[8,1,128]{2,1,0:T(1,128)} %broadcast_in_dim.18), calls=%async_computation.4 | async-start | bytes 8192 | tf_op jit(solution)/shard_map/all_to_all | solution.py:12
  291.7 100.9 %all-gather.6.cloned.1.call-start = ((), (), s32[]{:S(2)}) async-start(), calls=%async_computation.8 | async-start | bytes 6488064 | tf_op jit(solution)/shard_map/all_gather | solution.py:102
  297.7 9.3 %copy-start.6 = (bf16[128,512]{1,0:T(8,128)(2,1)}, bf16[128,512]{1,0:T(8,128)(2,1)S(1)}, u32[]{:S(2)}) copy-start(bf16[128,512]{1,0:T(8,128)(2,1)S(1)} %fusion.34) | copy-start | bytes 393220
Sparse Core Ops, SparseCore 0:
  80.5 54.0 all-gather.3
  165.9 61.0 reduce-scatter.1
  308.0 84.5 all-gather.5
where the time goes:
time: 414 us; the launch traced here: 413 us
  waiting for transfers between devices  232 us (56%)
  blocking collectives  55.6 us (13%)
  matrix products  36.5 us (9%)
  local copies, waits for them, and re-layouts  31.6 us (8%)
  other arithmetic  23.5 us (6%)
  starting transfers between devices  19.9 us (5%)
  between operations  14.6 us (4%)
    all_gather x1, waiting for transfers between devices, shards(): lax.all_gather(suffix_grad, 'expert', axis=0, tiled=True)  84.7 us
    reduce_scatter x1, waiting for transfers between devices, shards(): lax.psum_scatter(partial_rounded, 'vocab', scatter_dimension=1, tiled=True)  55.1 us
    all_gather x1, waiting for transfers between devices, shards(): incoming = lax.all_gather(arrived, 'vocab', axis=1, tiled=True)  54.2 us
    all_to_all x1, blocking collectives, shards(): lax.all_to_all(buffer, 'expert', split_axis=0, concat_axis=0, tiled=True)  46.4 us
    all_to_all x1, waiting for transfers between devices, shards(): lax.all_to_all(slot_grad.astype(jnp.bfloat16), 'expert', split_axis=0, co...  34.5 us
    dot_general x1, matrix products, shards(): lax.dot_general(up_grad, up_weight[0], contract, preferred_element_type=j...  14.2 us
    unnamed x21, local copies, waits for them, and re-layouts  11.4 us
    all_to_all x1, starting transfers between devices, shards(): lax.all_to_all(slot_grad.astype(jnp.bfloat16), 'expert', split_axis=0, co...  10.2 us
  transfers between devices with their start and end apart: 6, of which 5 were waited for; matrix products, arithmetic and copies ran while one was open for 0% of the time, Pallas kernels for 0%

commit v1 on v0

--- a/solution.py
+++ b/solution.py
@@ -5,6 +5,12 @@
 
 D = 4096
 SUFFIX = 20
+
+
+def tiled_gather(x, axis, dim):
+    devices = lax.axis_size(axis)
+    repeats = [devices if d == dim else 1 for d in range(x.ndim)]
+    return lax.all_to_all(jnp.tile(x, repeats), axis, split_axis=dim, concat_axis=dim, tiled=True)
 
 
 def sent_to_all(value, axis):
@@ -99,7 +105,7 @@
     suffix_grad = lax.dynamic_slice_in_dim(token_grad, suffix_start[0], SUFFIX, 0)
     suffix_grad = collect(suffix_grad, "vocab", 1)
     raw_scores = -lax.dot_general(
-        lax.all_gather(suffix_grad, "expert", axis=0, tiled=True),
+        tiled_gather(suffix_grad, "expert", 0),
         embedding,
         contract,
         preferred_element_type=jnp.float32,

time: 414 us -> 479 us (1.16)
  waiting for transfers between devices: 232 us -> 288 us
  starting transfers between devices: 19.9 us -> 26 us
    all_to_all x0 -> x1, waiting for transfers between devices: none -> 141 us  [tiled_gather(): lax.all_to_all(jnp.tile(x, repeats), axis, split_axis=dim, concat_axis=di...]
    all_gather x1 -> x0, waiting for transfers between devices: 84.7 us -> none  [shards(): lax.all_gather(suffix_grad, 'expert', axis=0, tiled=True)]
    unnamed x21, local copies, waits for them, and re-layouts: 11.4 us -> 2.87 us
    all_to_all x0 -> x1, local copies, waits for them, and re-layouts: none -> 7.84 us  [tiled_gather(): lax.all_to_all(jnp.tile(x, repeats), axis, split_axis=dim, concat_axis=di...]
    all_to_all x0 -> x1, starting transfers between devices: none -> 6.05 us  [tiled_gather(): lax.all_to_all(jnp.tile(x, repeats), axis, split_axis=dim, concat_axis=di...]
where the time goes in v1:
time: 479 us; the launch traced here: 477 us
  waiting for transfers between devices  288 us (60%)
  blocking collectives  55.6 us (12%)
  matrix products  36.5 us (8%)
  local copies, waits for them, and re-layouts  34.3 us (7%)
  starting transfers between devices  26 us (5%)
  other arithmetic  22.3 us (5%)
  between operations  14.9 us (3%)
    all_to_all x1, waiting for transfers between devices, tiled_gather(): lax.all_to_all(jnp.tile(x, repeats), axis, split_axis=dim, concat_axis=di...  141 us
    reduce_scatter x1, waiting for transfers between devices, shards(): lax.psum_scatter(partial_rounded, 'vocab', scatter_dimension=1, tiled=True)  55.1 us
    all_gather x1, waiting for transfers between devices, shards(): incoming = lax.all_gather(arrived, 'vocab', axis=1, tiled=True)  54.2 us
    all_to_all x1, blocking collectives, shards(): lax.all_to_all(buffer, 'expert', split_axis=0, concat_axis=0, tiled=True)  46.4 us
    all_to_all x1, waiting for transfers between devices, shards(): lax.all_to_all(slot_grad.astype(jnp.bfloat16), 'expert', split_axis=0, co...  34.5 us
    dot_general x1, matrix products, shards(): lax.dot_general(up_grad, up_weight[0], contract, preferred_element_type=j...  14.2 us
    all_to_all x1, starting transfers between devices, shards(): lax.all_to_all(slot_grad.astype(jnp.bfloat16), 'expert', split_axis=0, co...  10.2 us
    all_to_all x2, starting transfers between devices, sent_to_all(): lax.all_to_all(jnp.broadcast_to(value[None], (peers, *value.shape)), axis...  9.67 us
  transfers between devices with their start and end apart: 6, of which 5 were waited for; matrix products, arithmetic and copies ran while one was open for 0% of the time, Pallas kernels for 0%

profile of v1, /device:TPU:8, one launch (start us, length us, event | category | flops | bytes accessed | tf_op | source)
XLA Modules:
  0.0 477.1 jit_solution(7408411396727869910)
XLA Ops:
  7.2 0.9 copy.37
  8.2 0.1 eq.29
  8.3 0.1 eq.25
  8.3 0.7 broadcast_multiply_fusion
  9.1 9.0 %reduce-window.6 = s32[32,8,128]{2,1,0:T(8,128)S(1)} reduce-window(s32[32,8,128]{2,1,0:T(8,128)S(1)} %fusion.39, s32[]{:T(128)} %constant.7.clone.1), window={size=1x1x128 pad=0_0x0_0x127_0}, to_apply=%region_2.3 | reduce-window | flops 4161536 | bytes 262148 | tf_op jit(solution)/shard_map/reduce-window
  18.1 0.1 slice.10
  18.2 0.1 copy.39
  18.3 0.1 copy.40
  18.4 0.1 broadcast_add_fusion
  18.5 0.1 copy.36
  18.6 0.1 mul.95
  18.7 0.9 convert_element_type.50
  19.7 0.7 reduce_sum.69
  20.4 0.7 broadcast_divide_fusion
  21.0 0.7 copy.41
  21.8 0.9 mul.97
  22.8 6.6 %scatter_custom_fusion = bf16[1216,512]{1,0:T(8,128)(2,1)} fusion(s32[1024]{0:T(1024)S(1)} %bitcast.71, f32[128,512]{1,0:T(8,128)S(1)} %convert_element_type.50, f32[1024]{0:T(1024)S(1)} %mul.97, bf16[]{:T(256)} %constant.5.clone.1), kind=kCustom, calls=%fused_computation.16 | custom fusion | flops 1048576 | bytes 1511426 | tf_op jit(solution)/shard_map/scatter | solution.py:69
  29.4 2.3 all_to_all.32
  31.7 46.4 %all_to_all.47 = bf16[32,38,512]{2,1,0:T(8,128)(2,1)} all-to-all(bf16[32,38,512]{2,1,0:T(8,128)(2,1)} %all_to_all.32), channel_id=1, replica_groups=mesh['expert'=32,'vocab'=8] {'expert'}, dimensions={0} | all-to-all | bytes 2490368 | tf_op jit(solution)/shard_map/all_to_all | solution.py:70
  78.1 2.3 all_to_all.34
  80.4 54.2 %all-gather.2.cloned.1.call-done = bf16[1216,4096]{1,0:T(8,128)(2,1)} async-done(((bf16[1216,512]{1,0:T(8,128)(2,1)}), bf16[1216,4096]{1,0:T(8,128)(2,1)}) %all-gather.2.cloned.1.call-update) | async-done | bytes 9961488 | tf_op jit(solution)/shard_map/all_gather | solution.py:71
  134.6 7.6 %fusion.4 = f32[1216,192]{0,1:T(8,128)S(1)} fusion(bf16[1216,4096]{1,0:T(8,128)(2,1)} %all-gather.2.cloned.1.call-done, bf16[1,192,4096]{2,1,0:T(8,128)(2,1)} %param.22), kind=kOutput, calls=%fused_computation.9 | convolution fusion | flops 1912602624 | bytes 12468224 | tf_op jit(solution)/shard_map/dot_general | solution.py:72
  142.2 0.9 copy-done.1
  143.2 8.4 %fusion.2 = f32[1216,4096]{1,0:T(8,128)} fusion(bf16[1,4096,192]{1,2,0:T(8,128)(2,1)S(1)} %copy-done.3, f32[1216,192]{0,1:T(8,128)S(1)} %fusion.4, bf16[1,1216,192]{1,2,0:T(8,128)(2,1)S(1)} %copy-done.5, bf16[1,1216,192]{1,2,0:T(8,128)(2,1)S(1)} %copy-done.2), kind=kOutput, calls=%fused_computation.7 | convolution fusion | flops 1915404288 | bytes 23363584 | tf_op jit(solution)/shard_map/dot_general | solution.py:82
  151.6 14.2 %add_convert_fusion = bf16[1216,4096]{1,0:T(8,128)(2,1)} fusion(f32[1216,4096]{1,0:T(8,128)} %fusion.2, bf16[1,4096,192]{1,2,0:T(8,128)(2,1)} %param.21, f32[1216,192]{0,1:T(8,128)} %copy-done.1, bf16[1,1216,192]{1,2,0:T(8,128)(2,1)} %param.18), kind=kOutput, calls=%fused_computation.2 | convolution fusion | flops 1924198400 | bytes 32858112 | tf_op jit(solution)/shard_map/dot_general | solution.py:85
  165.7 0.9 copy-done.4
  166.6 0.1 fusion.35
  166.7 0.6 broadcast_in_dim.16
  167.3 4.5 all-to-all-start
  171.9 55.1 %reduce-scatter.2.cloned.1.call-done = bf16[1216,512]{1,0:T(8,128)(2,1)} async-done(((bf16[1216,4096]{1,0:T(8,128)(2,1)}), bf16[1216,512]{1,0:T(8,128)(2,1)}) %reduce-scatter.2.cloned.1.call-update) | async-done | bytes 1245200 | tf_op jit(solution)/shard_map/reduce_scatter | solution.py:89
  227.0 2.3 all_to_all.35
  229.3 10.2 %all-to-all-start.2 = ((bf16[32,38,512]{2,1,0:T(8,128)(2,1)}), bf16[32,38,512]{2,1,0:T(8,128)(2,1)}, u32[]{:S(2)}, u32[]{:S(2)}) async-start(bf16[32,38,512]{2,1,0:T(8,128)(2,1)} %all_to_all.35), calls=%async_computation.3 | async-start | bytes 2621440 | tf_op jit(solution)/shard_map/all_to_all | solution.py:92
  239.5 34.5 %all-to-all-done.2 = bf16[32,38,512]{2,1,0:T(8,128)(2,1)} async-done(((bf16[32,38,512]{2,1,0:T(8,128)(2,1)}), bf16[32,38,512]{2,1,0:T(8,128)(2,1)}, u32[]{:S(2)}, u32[]{:S(2)}) %all-to-all-start.2) | async-done | bytes 1245216 | tf_op jit(solution)/shard_map/all_to_all | solution.py:92
  274.0 2.7 reshape.105
  276.7 7.0 %gather_fusion = f32[1024,512]{1,0:T(8,128)} fusion(f32[1216,512]{1,0:T(8,128)} %reshape.105, s32[1024]{0:T(1024)S(1)} %broadcast_clamp_fusion), kind=kCustom, calls=%fused_computation | custom fusion | bytes 4198400 | tf_op jit(solution)/shard_map/gather | solution.py:95
  283.6 2.1 bitcast_reduce_fusion
  285.8 0.2 fusion.30
  285.9 0.6 broadcast_in_dim.18
  286.5 5.1 %all-to-all-start.3 = ((f32[8,1,128]{2,1,0:T(1,128)}), f32[8,1,128]{2,1,0:T(1,128)S(1)}, u32[]{:S(2)}, u32[]{:S(2)}) async-start(f32[8,1,128]{2,1,0:T(1,128)} %broadcast_in_dim.18), calls=%async_computation.4 | async-start | bytes 8192 | tf_op jit(solution)/shard_map/all_to_all | solution.py:18
  292.3 3.1 all-to-all-done.3
  295.5 1.1 fusion.34
  296.6 9.2 %all_to_all.48 = bf16[8,20,512]{2,1,0:T(8,128)(2,1)S(1)} all-to-all(bf16[8,20,512]{2,1,0:T(8,128)(2,1)S(1)} %broadcast_in_dim.20), channel_id=1, replica_groups=mesh['expert'=32,'vocab'=8] {'vocab'}, dimensions={0} | all-to-all | bytes 327680 | tf_op jit(solution)/shard_map/all_to_all | solution.py:18
  305.9 0.1 copy.45
  306.0 3.4 tile.9
  309.4 6.0 %all-to-all-start.5 = ((bf16[32,20,4096]{2,1,0:T(8,128)(2,1)}), bf16[32,20,4096]{2,1,0:T(8,128)(2,1)}, u32[]{:S(2)}, u32[]{:S(2)}) async-start(bf16[32,20,4096]{2,1,0:T(8,128)(2,1)} %tile.9), calls=%async_computation.6 | async-start | bytes 12582912 | tf_op jit(solution)/shard_map/all_to_all | solution.py:13
  315.5 140.7 %all-to-all-done.5 = bf16[32,20,4096]{2,1,0:T(8,128)(2,1)} async-done(((bf16[32,20,4096]{2,1,0:T(8,128)(2,1)}), bf16[32,20,4096]{2,1,0:T(8,128)(2,1)}, u32[]{:S(2)}, u32[]{:S(2)}) %all-to-all-start.5) | async-done | bytes 5242912 | tf_op jit(solution)/shard_map/all_to_all | solution.py:13
  456.1 7.8 %all_to_all.40 = bf16[640,4096]{1,0:T(8,128)(2,1)} reshape(bf16[32,20,4096]{2,1,0:T(8,128)(2,1)} %all-to-all-done.5) | data formatting | bytes 10485760 | tf_op jit(solution)/shard_map/all_to_all | solution.py:13
  464.0 6.3 %fusion.6 = f32[640,384]{1,0:T(8,128)} fusion(bf16[640,4096]{1,0:T(8,128)(2,1)} %all_to_all.40, bf16[384,4096]{1,0:T(8,128)(2,1)S(1)} %copy-done, pred[384]{0:T(512)(128)(4,1)S(1)} %broadcast_compare_fusion), kind=kOutput, calls=%fused_computation.15 | convolution fusion | flops 2013757440 | bytes 9372032 | tf_op jit(solution)/shard_map/dot_general | solution.py:107
  (36 shorter events, 0.4 us)
Async XLA Ops:
  7.2 456.8 %copy-start = (bf16[384,4096]{1,0:T(8,128)(2,1)S(1)}, bf16[384,4096]{1,0:T(8,128)(2,1)}, u32[]{:S(2)}) copy-start(bf16[384,4096]{1,0:T(8,128)(2,1)} %param.23) | copy-start | bytes 9437188
  7.2 127.4 %all-gather.2.cloned.1.call-start = ((), (), s32[]{:S(2)}) async-start(), calls=%async_computation.7 | async-start | bytes 11206656 | tf_op jit(solution)/shard_map/all_gather | solution.py:71
  80.4 146.6 %reduce-scatter.2.cloned.1.call-start = ((), (), s32[]{:S(2)}) async-start(), calls=%async_computation.8 | async-start | bytes 11206656 | tf_op jit(solution)/shard_map/reduce_scatter | solution.py:89
  134.6 8.6 %copy-start.2 = (bf16[1,1216,192]{1,2,0:T(8,128)(2,1)S(1)}, bf16[1,1216,192]{1,2,0:T(8,128)(2,1)}, u32[]{:S(2)}) copy-start(bf16[1,1216,192]{1,2,0:T(8,128)(2,1)} %param.18) | copy-start | bytes 1400836
  134.6 8.6 %copy-start.3 = (bf16[1,4096,192]{1,2,0:T(8,128)(2,1)S(1)}, bf16[1,4096,192]{1,2,0:T(8,128)(2,1)}, u32[]{:S(2)}) copy-start(bf16[1,4096,192]{1,2,0:T(8,128)(2,1)} %param.20) | copy-start | bytes 4718596
  134.6 8.6 %copy-start.5 = (bf16[1,1216,192]{1,2,0:T(8,128)(2,1)S(1)}, bf16[1,1216,192]{1,2,0:T(8,128)(2,1)}, u32[]{:S(2)}) copy-start(bf16[1,1216,192]{1,2,0:T(8,128)(2,1)} %param.19) | copy-start | bytes 1400836
  142.2 0.9 copy-start.1
  165.7 0.9 copy-start.4
  167.3 62.0 %all-to-all-start = ((f32[8,1,128]{2,1,0:T(1,128)}), f32[8,1,128]{2,1,0:T(1,128)S(1)}, u32[]{:S(2)}, u32[]{:S(2)}) async-start(f32[8,1,128]{2,1,0:T(1,128)} %broadcast_in_dim.16), calls=%async_computation | async-start | bytes 8192 | tf_op jit(solution)/shard_map/all_to_all | solution.py:18
  229.3 44.7 %all-to-all-start.2 = ((bf16[32,38,512]{2,1,0:T(8,128)(2,1)}), bf16[32,38,512]{2,1,0:T(8,128)(2,1)}, u32[]{:S(2)}, u32[]{:S(2)}) async-start(bf16[32,38,512]{2,1,0:T(8,128)(2,1)} %all_to_all.35), calls=%async_computation.3 | async-start | bytes 2621440 | tf_op jit(solution)/shard_map/all_to_all | solution.py:92
  283.6 2.1 copy-start.7
  286.5 8.9 %all-to-all-start.3 = ((f32[8,1,128]{2,1,0:T(1,128)}), f32[8,1,128]{2,1,0:T(1,128)S(1)}, u32[]{:S(2)}, u32[]{:S(2)}) async-start(f32[8,1,128]{2,1,0:T(1,128)} %broadcast_in_dim.18), calls=%async_computation.4 | async-start | bytes 8192 | tf_op jit(solution)/shard_map/all_to_all | solution.py:18
  296.5 9.4 %copy-start.6 = (bf16[128,512]{1,0:T(8,128)(2,1)}, bf16[128,512]{1,0:T(8,128)(2,1)S(1)}, u32[]{:S(2)}) copy-start(bf16[128,512]{1,0:T(8,128)(2,1)S(1)} %fusion.34) | copy-start | bytes 393220
  309.4 6.1 %copy-start.8 = (s32[384]{0:T(512)S(1)}, s32[384]{0:T(512)}, u32[]{:S(2)}) copy-start(s32[384]{0:T(512)} %param.24) | copy-start | bytes 4612
  309.4 146.7 %all-to-all-start.5 = ((bf16[32,20,4096]{2,1,0:T(8,128)(2,1)}), bf16[32,20,4096]{2,1,0:T(8,128)(2,1)}, u32[]{:S(2)}, u32[]{:S(2)}) async-start(bf16[32,20,4096]{2,1,0:T(8,128)(2,1)} %tile.9), calls=%async_computation.6 | async-start | bytes 12582912 | tf_op jit(solution)/shard_map/all_to_all | solution.py:13
Sparse Core Ops, SparseCore 0:
  80.5 54.0 all-gather.1
  165.9 61.0 reduce-scatter.1
